TPU v7x, 256 devices: a whole 4x4x8 slice. The times are simulated.
256 devices in a mesh: scen: 16 (over z_lo, y, core), tm: 16 (over z_hi, x).
Axes of the slice: x: 4, y: 4, z: 8 (z_hi: 4, z_lo: 2; z = z_hi * 2 + z_lo), core: 2. Of those that a mesh axis runs over, the one named last changes fastest.
Arguments:
- cotangent: float32 [64, 336, 2048], P('scen', 'tm'), may hold values from -6 to 6
- blocks: bfloat16 [16, 6, 128, 128], P('tm'), may hold values from -0.21875 to 0.21875
- zone_links: int32 [16, 6], replicated, may hold values from 0 to 15, as said below
- step_size: float32 [2048], replicated, may hold values from 0.3 to 1
- coupling: bfloat16 [16, 336, 336], P('tm'), may hold values from -0.3125 to 0.3125
- ramp_band: int32 [16], P('tm'), may hold values from 42 to 336, as said below
- candidates: int32 [2048], P('scen'), may hold values from 0 to 2047, as said below
Outputs:
- initial_adjoint: float32 [64, 336, 2048], P('scen', 'tm')
- siting_gradient: float32 [336, 2048], P('tm', 'scen')
Inputs may be any that keep to these rules, and one draw needn't show every extreme that they name: zone_links[z, 0] = z, and the 6 entries of a row are distinct zones. `ramp_band`: at least one zone has reach 336. `candidates`: the entries of block m of 128 consecutive entries are distinct buses in m * (128) to (m + 1) * 128 - 1.
All inputs are finite; a program needn't handle non-finite values.
Results may differ from a plain program's by a relative error of at most 0.0029.
Values may be sent and summed in bfloat16 or wider, within the bound.
No kernel may reach another device: no remote copies, remote signals or barrier semaphores. Data moves between devices by JAX's collectives and lax.ppermute only.
A program may use at most 64 MiB of HBM per device.

v0:
```python
import jax
import jax.numpy as jnp
from jax import lax
from jax.sharding import PartitionSpec as P

SWEEPS = 2


def network_term(scaled, link_blocks, zone_links):
    scen_count, hour_count, buses = scaled.shape
    link_count, zone_count, bus_width = (
        link_blocks.shape[0],
        link_blocks.shape[1],
        link_blocks.shape[3],
    )
    zone_major = jnp.transpose(
        scaled.reshape(scen_count * hour_count, zone_count, bus_width), (1, 0, 2)
    )
    total = jnp.zeros((zone_count, scen_count * hour_count, bus_width), jnp.float32)
    for link in range(link_count):
        picked = jnp.take(zone_major, zone_links[:, link], axis=0)
        total = total + lax.dot_general(
            picked,
            link_blocks[link],
            (((2,), (1,)), ((0,), (0,))),
            preferred_element_type=jnp.float32,
        )
    return jnp.transpose(total, (1, 0, 2)).reshape(scen_count, hour_count, buses)


def temporal_term(moved, masked_turned):
    scen_count, hour_count, owned = moved.shape
    zone_count = masked_turned.shape[0]
    bus_width = owned // zone_count
    rows = []
    for scen in range(scen_count):
        column = moved[scen, :, 0:bus_width]
        pieces = jnp.dot(masked_turned[0], column, preferred_element_type=jnp.float32)
        rows.append(pieces)
    return jnp.stack(rows, axis=0).astype(jnp.bfloat16)


def per_device(cotangent, blocks, zone_links, step_size, coupling, ramp_band, candidates):
    all_blocks = lax.all_gather(blocks, "tm", axis=0, tiled=True)
    link_blocks = jnp.transpose(all_blocks, (1, 0, 2, 3))
    hour_count = coupling.shape[1]
    hour_ids = jnp.arange(hour_count, dtype=jnp.int32)
    spread = jnp.abs(hour_ids[:, None] - hour_ids[None, :])
    masked = jnp.where(
        spread[None, :, :] <= ramp_band[:, None, None], coupling, jnp.zeros_like(coupling)
    )
    masked_turned = jnp.transpose(masked, (0, 2, 1))
    scen_total = cotangent.shape[0] * lax.axis_size("scen")
    adjoint = cotangent
    grad_local = jnp.zeros((cotangent.shape[1], cotangent.shape[2]), jnp.float32)
    for sweep in range(SWEEPS):
        weighted = adjoint * step_size[None, None, :]
        sweep_grad = jnp.sum(weighted, axis=0) * (1.0 / scen_total)
        grad_local = grad_local + sweep_grad
        scaled = weighted.astype(jnp.bfloat16)
        moved = lax.all_to_all(scaled, "tm", split_axis=2, concat_axis=1, tiled=True)
        temporal = lax.all_to_all(
            temporal_term(moved, masked_turned), "tm", split_axis=1, concat_axis=2, tiled=True
        )
        network = network_term(scaled, link_blocks, zone_links)
        adjoint = adjoint - network - temporal.astype(jnp.float32)
    reduced = lax.psum_scatter(grad_local, "scen", scatter_dimension=1, tiled=True)
    width = reduced.shape[1]
    local_cols = candidates - lax.axis_index("scen") * width
    siting_gradient = jnp.take(reduced, local_cols, axis=1)
    return (adjoint, siting_gradient)


def solution(mesh):
    placed = (
        P("scen", "tm", None),
        P("tm", None, None, None),
        P(),
        P(),
        P("tm", None, None),
        P("tm"),
        P("scen"),
    )
    return jax.shard_map(
        per_device,
        mesh=mesh,
        in_specs=placed,
        out_specs=(P("scen", "tm", None), P("tm", "scen")),
        check_vma=False,
    )
```

profile of v0, /device:TPU:24, one launch (start us, length us, event | category | flops | bytes accessed | tf_op | source)
XLA Modules:
  0.0 205.9 jit_solution(9475349268298341223)
XLA Ops:
  10.9 4.2 %reshape.228 = bf16[16,2,5376]{2,1,0:T(2,128)(2,1)} reshape(bf16[2048,4,21]{2,1,0:T(4,128)(2,1)S(1)} %bitcast.148) | data formatting | bytes 688128
  15.0 11.0 %all-to-all-start = ((bf16[16,2,5376]{2,1,0:T(2,128)(2,1)}), bf16[16,2,5376]{2,1,0:T(2,128)(2,1)S(1)}, u32[]{:S(2)}, u32[]{:S(2)}) async-start(bf16[16,2,5376]{2,1,0:T(2,128)(2,1)} %reshape.228), calls=%async_computation | async-start | bytes 688128 | tf_op jit(solution)/shard_map/all_to_all | solution.py:61
  27.2 14.7 %all-to-all-done = bf16[16,2,5376]{2,1,0:T(2,128)(2,1)S(1)} async-done(((bf16[16,2,5376]{2,1,0:T(2,128)(2,1)}), bf16[16,2,5376]{2,1,0:T(2,128)(2,1)S(1)}, u32[]{:S(2)}, u32[]{:S(2)}) %all-to-all-start) | async-done | bytes 344096 | tf_op jit(solution)/shard_map/all_to_all | solution.py:61
  41.9 5.1 %reshape.229 = bf16[2048,4,21]{2,1,0:T(4,128)(2,1)S(1)} reshape(bf16[16,2,5376]{2,1,0:T(2,128)(2,1)S(1)} %all-to-all-done) | data formatting | bytes 688128
  50.9 6.2 %all-to-all-start.1 = ((bf16[4,336,128]{2,0,1:T(4,128)(2,1)}), bf16[4,336,128]{2,0,1:T(4,128)(2,1)S(1)}, u32[]{:S(2)}, u32[]{:S(2)}) async-start(bf16[4,336,128]{2,0,1:T(4,128)(2,1)} %copy.93), calls=%async_computation.1 | async-start | bytes 688128 | tf_op jit(solution)/shard_map/all_to_all | solution.py:62
  65.9 6.9 %all-to-all-done.1 = bf16[4,336,128]{2,0,1:T(4,128)(2,1)S(1)} async-done(((bf16[4,336,128]{2,0,1:T(4,128)(2,1)}), bf16[4,336,128]{2,0,1:T(4,128)(2,1)S(1)}, u32[]{:S(2)}, u32[]{:S(2)}) %all-to-all-start.1) | async-done | bytes 344096 | tf_op jit(solution)/shard_map/all_to_all | solution.py:62
  73.9 13.9 %all-gather.2.cloned.1.call-done = bf16[16,6,128,128]{3,2,0,1:T(8,128)(2,1)} async-done(((bf16[1,6,128,128]{3,2,0,1:T(8,128)(2,1)}), bf16[16,6,128,128]{3,2,0,1:T(8,128)(2,1)}) %all-gather.2.cloned.1.call-update) | async-done | bytes 3145744 | tf_op jit(solution)/shard_map/all_gather | solution.py:44
  87.8 1.7 fusion.15
  94.8 2.1 %reshape.78 = f32[4,21,2048]{2,1,0:T(8,128)} reshape(f32[84,16,128]{2,1,0:T(8,128)} %copy.85) | data formatting | bytes 1376256 | tf_op jit(solution)/shard_map/reshape | solution.py:28
  96.9 2.9 %multiply_reduce_fusion = (f32[21,2048]{1,0:T(8,128)}, f32[21,2048]{1,0:T(8,128)}, f32[4,21,2048]{2,1,0:T(8,128)S(1)}) fusion(f32[2048]{0:T(1024)S(1)} %copy-done.7, f32[4,21,2048]{2,0,1:T(4,128)} %param.9, f32[4,21,2048]{2,1,0:T(8,128)} %reshape.226, f32[4,21,2048]{2,1,0:T(8,128)} %reshape.78), kind=kLoop, calls=%fused_computation.47 | loop fusion | flops 946176 | bytes 3104768 | tf_op jit(solution)/shard_map/reduce_sum | solution.py:58
  109.3 4.0 %copy.98 = bf16[4,21,2048]{1,0,2:T(4,128)(2,1)} copy(bf16[4,21,2048]{2,1,0:T(8,128)(2,1)} %copy-done.3) | data formatting | bytes 688128 | tf_op jit(solution)/shard_map/convert_element_type | solution.py:60
  113.3 1.7 add_multiply_fusion
  115.1 2.2 %fusion.14 = f32[16,84,128]{2,1,0:T(8,128)} fusion(bf16[6,16,128,128]{3,2,1,0:T(8,128)(2,1)S(1)} %bitcast.139, bf16[16,84,128]{2,1,0:T(8,128)(2,1)} %gather_fusion.7, pred[16]{0:T(512)(128)(4,1)S(1)} %copy-done.23), kind=kOutput, calls=%fused_computation.59 | convolution fusion | flops 44212224 | bytes 1556992 | tf_op jit(solution)/shard_map/dot_general | solution.py:22
  117.3 5.1 %reshape.230 = bf16[16,2,5376]{2,1,0:T(2,128)(2,1)} reshape(bf16[2048,4,21]{2,1,0:T(4,128)(2,1)} %bitcast.145) | data formatting | bytes 688128
  122.5 12.0 %all-to-all-start.2 = ((bf16[16,2,5376]{2,1,0:T(2,128)(2,1)}), bf16[16,2,5376]{2,1,0:T(2,128)(2,1)}, u32[]{:S(2)}, u32[]{:S(2)}) async-start(bf16[16,2,5376]{2,1,0:T(2,128)(2,1)} %reshape.230), calls=%async_computation.2 | async-start | bytes 688128 | tf_op jit(solution)/shard_map/all_to_all | solution.py:61
  134.5 2.5 %convolution_add_fusion.4 = f32[16,84,128]{2,1,0:T(8,128)} fusion(f32[16,84,128]{2,1,0:T(8,128)} %fusion.14, bf16[6,16,128,128]{3,2,1,0:T(8,128)(2,1)S(1)} %bitcast.140, bf16[16,84,128]{2,1,0:T(8,128)(2,1)} %gather_fusion.8, pred[16]{0:T(512)(128)(4,1)S(1)} %copy-done.21), kind=kOutput, calls=%fused_computation.18 | convolution fusion | flops 44384256 | bytes 2245120 | tf_op jit(solution)/shard_map/dot_general | solution.py:22
  138.3 1.6 convolution_add_fusion.3
  140.0 2.2 %convolution_add_fusion.2 = f32[16,84,128]{2,1,0:T(8,128)} fusion(f32[16,84,128]{2,1,0:T(8,128)S(1)} %convolution_add_fusion.3, bf16[6,16,128,128]{3,2,1,0:T(8,128)(2,1)S(1)} %bitcast.142, bf16[16,84,128]{2,1,0:T(8,128)(2,1)} %gather_fusion.10, pred[16]{0:T(512)(128)(4,1)S(1)} %copy-done.17), kind=kOutput, calls=%fused_computation.16 | convolution fusion | flops 44384256 | bytes 2277888 | tf_op jit(solution)/shard_map/dot_general | solution.py:22
  142.2 6.9 %all-to-all-done.2 = bf16[16,2,5376]{2,1,0:T(2,128)(2,1)} async-done(((bf16[16,2,5376]{2,1,0:T(2,128)(2,1)}), bf16[16,2,5376]{2,1,0:T(2,128)(2,1)}, u32[]{:S(2)}, u32[]{:S(2)}) %all-to-all-start.2) | async-done | bytes 344096 | tf_op jit(solution)/shard_map/all_to_all | solution.py:61
  149.1 7.1 %reshape.231 = bf16[2048,4,21]{2,1,0:T(4,128)(2,1)} reshape(bf16[16,2,5376]{2,1,0:T(2,128)(2,1)} %all-to-all-done.2) | data formatting | bytes 688128
  156.2 3.4 %copy.112 = bf16[4,21,16,128]{3,2,0,1:T(8,128)(2,1)} copy(bf16[4,21,16,128]{1,0,3,2:T(4,128)(2,1)} %bitcast.147) | data formatting | bytes 688128 | tf_op jit(solution)/shard_map/all_to_all | solution.py:61
  159.6 1.7 fusion.74
  162.0 1.6 squeeze.99
  163.6 1.6 copy.101
  165.2 1.6 squeeze.100
  166.7 1.6 copy.102
  168.3 1.6 squeeze.101
  171.4 1.6 squeeze.102
  179.2 4.2 %all-to-all-start.3 = ((bf16[4,336,128]{2,0,1:T(4,128)(2,1)}), bf16[4,336,128]{2,0,1:T(4,128)(2,1)}, u32[]{:S(2)}, u32[]{:S(2)}) async-start(bf16[4,336,128]{2,0,1:T(4,128)(2,1)} %copy.104), calls=%async_computation.3 | async-start | bytes 688128 | tf_op jit(solution)/shard_map/all_to_all | solution.py:62
  183.4 2.5 %convolution_add_fusion.1 = f32[16,84,128]{2,1,0:T(8,128)} fusion(f32[16,84,128]{2,1,0:T(8,128)} %convolution_add_fusion.2, bf16[6,16,128,128]{3,2,1,0:T(8,128)(2,1)S(1)} %bitcast.143, bf16[16,84,128]{2,1,0:T(8,128)(2,1)} %gather_fusion.11, pred[16]{0:T(512)(128)(4,1)S(1)} %copy-done.15), kind=kOutput, calls=%fused_computation.15 | convolution fusion | flops 44384256 | bytes 2245120 | tf_op jit(solution)/shard_map/dot_general | solution.py:22
  187.2 1.6 fusion
  191.5 4.9 %all-to-all-done.3 = bf16[4,336,128]{2,0,1:T(4,128)(2,1)} async-done(((bf16[4,336,128]{2,0,1:T(4,128)(2,1)}), bf16[4,336,128]{2,0,1:T(4,128)(2,1)}, u32[]{:S(2)}, u32[]{:S(2)}) %all-to-all-start.3) | async-done | bytes 344096 | tf_op jit(solution)/shard_map/all_to_all | solution.py:62
  (130 shorter events, 48.7 us)
Async XLA Ops:
  7.2 80.6 %all-gather.2.cloned.1.call-start = ((), (), s32[]{:S(2)}) async-start(), calls=%async_computation.5 | async-start | bytes 3342336 | tf_op jit(solution)/shard_map/all_gather | solution.py:44
  9.4 17.7 %copy-start.24 = (s32[16,6]{0,1:T(8,128)S(1)}, s32[16,6]{0,1:T(8,128)}, u32[]{:S(2)}) copy-start(s32[16,6]{0,1:T(8,128)} %param.11) | copy-start | bytes 1156
  15.0 26.9 %all-to-all-start = ((bf16[16,2,5376]{2,1,0:T(2,128)(2,1)}), bf16[16,2,5376]{2,1,0:T(2,128)(2,1)S(1)}, u32[]{:S(2)}, u32[]{:S(2)}) async-start(bf16[16,2,5376]{2,1,0:T(2,128)(2,1)} %reshape.228), calls=%async_computation | async-start | bytes 688128 | tf_op jit(solution)/shard_map/all_to_all | solution.py:61
  27.1 60.7 %copy-start.22 = (pred[16]{0:T(512)(128)(4,1)}, pred[16]{0:T(512)(128)(4,1)S(1)}, u32[]{:S(2)}) copy-start(pred[16]{0:T(512)(128)(4,1)S(1)} %get-tuple-element.44) | copy-start | bytes 52
  27.1 62.4 %copy-start.20 = (pred[16]{0:T(512)(128)(4,1)}, pred[16]{0:T(512)(128)(4,1)S(1)}, u32[]{:S(2)}) copy-start(pred[16]{0:T(512)(128)(4,1)S(1)} %get-tuple-element.42) | copy-start | bytes 52
  27.1 63.9 %copy-start.18 = (pred[16]{0:T(512)(128)(4,1)}, pred[16]{0:T(512)(128)(4,1)S(1)}, u32[]{:S(2)}) copy-start(pred[16]{0:T(512)(128)(4,1)S(1)} %get-tuple-element.40) | copy-start | bytes 52
  27.1 65.4 %copy-start.16 = (pred[16]{0:T(512)(128)(4,1)}, pred[16]{0:T(512)(128)(4,1)S(1)}, u32[]{:S(2)}) copy-start(pred[16]{0:T(512)(128)(4,1)S(1)} %get-tuple-element.38) | copy-start | bytes 52
  27.1 65.8 %copy-start.14 = (pred[16]{0:T(512)(128)(4,1)}, pred[16]{0:T(512)(128)(4,1)S(1)}, u32[]{:S(2)}) copy-start(pred[16]{0:T(512)(128)(4,1)S(1)} %get-tuple-element.46) | copy-start | bytes 52
  27.1 66.2 %copy-start.12 = (pred[16]{0:T(512)(128)(4,1)}, pred[16]{0:T(512)(128)(4,1)S(1)}, u32[]{:S(2)}) copy-start(pred[16]{0:T(512)(128)(4,1)S(1)} %get-tuple-element.18) | copy-start | bytes 52
  27.2 21.6 %copy-start.27 = (bf16[1,336,336]{2,1,0:T(8,128)(2,1)S(1)}, bf16[1,336,336]{2,1,0:T(8,128)(2,1)}, u32[]{:S(2)}) copy-start(bf16[1,336,336]{2,1,0:T(8,128)(2,1)} %param.13) | copy-start | bytes 677380
  50.0 14.8 %copy-start.26 = (s32[128]{0:T(128)S(1)}, s32[128]{0:T(128)}, u32[]{:S(2)}) copy-start(s32[128]{0:T(128)} %param.15) | copy-start | bytes 1540
  50.9 21.9 %all-to-all-start.1 = ((bf16[4,336,128]{2,0,1:T(4,128)(2,1)}), bf16[4,336,128]{2,0,1:T(4,128)(2,1)S(1)}, u32[]{:S(2)}, u32[]{:S(2)}) async-start(bf16[4,336,128]{2,0,1:T(4,128)(2,1)} %copy.93), calls=%async_computation.1 | async-start | bytes 688128 | tf_op jit(solution)/shard_map/all_to_all | solution.py:62
  57.1 132.0 %reduce-scatter.2.cloned.1.call-start = ((), (), s32[]{:S(2)}) async-start(), calls=%async_computation.6 | async-start | bytes 208896 | tf_op jit(solution)/shard_map/reduce_scatter | solution.py:67
  57.4 15.5 %copy-start.8 = (s32[1024]{0:T(1024)}, s32[1024]{0:T(1024)S(1)}, u32[]{:S(2)}) copy-start(s32[1024]{0:T(1024)S(1)} %get-tuple-element.52) | copy-start | bytes 12292
  57.4 15.5 %copy-start.9 = (s32[1024]{0:T(1024)}, s32[1024]{0:T(1024)S(1)}, u32[]{:S(2)}) copy-start(s32[1024]{0:T(1024)S(1)} %get-tuple-element.53) | copy-start | bytes 12292
  59.4 14.5 %copy-start.10 = (s32[1024]{0:T(1024)}, s32[1024]{0:T(1024)S(1)}, u32[]{:S(2)}) copy-start(s32[1024]{0:T(1024)S(1)} %get-tuple-element.50) | copy-start | bytes 12292
  62.1 27.4 %copy-start.11 = (s32[1024]{0:T(1024)}, s32[1024]{0:T(1024)S(1)}, u32[]{:S(2)}) copy-start(s32[1024]{0:T(1024)S(1)} %get-tuple-element.49) | copy-start | bytes 12292
  87.8 3.2 %copy-start = (bf16[16,6,128,128]{3,2,0,1:T(8,128)(2,1)S(1)}, bf16[16,6,128,128]{3,2,0,1:T(8,128)(2,1)}, u32[]{:S(2)}) copy-start(bf16[16,6,128,128]{3,2,0,1:T(8,128)(2,1)} %all-gather.2.cloned.1.call-done) | copy-start | bytes 9437188
  87.8 4.7 %copy-start.4 = (bf16[16,84,128]{2,1,0:T(8,128)(2,1)S(1)}, bf16[16,84,128]{2,1,0:T(8,128)(2,1)}, u32[]{:S(2)}) copy-start(bf16[16,84,128]{2,1,0:T(8,128)(2,1)} %gather_fusion.4) | copy-start | bytes 1032196
  89.5 3.4 %copy-start.6 = (bf16[16,84,128]{2,1,0:T(8,128)(2,1)S(1)}, bf16[16,84,128]{2,1,0:T(8,128)(2,1)}, u32[]{:S(2)}) copy-start(bf16[16,84,128]{2,1,0:T(8,128)(2,1)} %gather_fusion.5) | copy-start | bytes 1032196
  91.1 2.3 %copy-start.5 = (bf16[16,84,128]{2,1,0:T(8,128)(2,1)S(1)}, bf16[16,84,128]{2,1,0:T(8,128)(2,1)}, u32[]{:S(2)}) copy-start(bf16[16,84,128]{2,1,0:T(8,128)(2,1)} %gather_fusion.6) | copy-start | bytes 1032196
  93.4 3.5 %copy-start.7 = (f32[2048]{0:T(1024)S(1)}, f32[2048]{0:T(1024)}, u32[]{:S(2)}) copy-start(f32[2048]{0:T(1024)} %param.12) | copy-start | bytes 24580
  103.5 11.6 %copy-start.23 = (pred[16]{0:T(512)(128)(4,1)S(1)}, pred[16]{0:T(512)(128)(4,1)}, u32[]{:S(2)}) copy-start(pred[16]{0:T(512)(128)(4,1)} %copy-done.22) | copy-start | bytes 52
  113.3 21.2 %copy-start.21 = (pred[16]{0:T(512)(128)(4,1)S(1)}, pred[16]{0:T(512)(128)(4,1)}, u32[]{:S(2)}) copy-start(pred[16]{0:T(512)(128)(4,1)} %copy-done.20) | copy-start | bytes 52
  117.3 21.0 %copy-start.19 = (pred[16]{0:T(512)(128)(4,1)S(1)}, pred[16]{0:T(512)(128)(4,1)}, u32[]{:S(2)}) copy-start(pred[16]{0:T(512)(128)(4,1)} %copy-done.18) | copy-start | bytes 52
  122.5 17.5 %copy-start.17 = (pred[16]{0:T(512)(128)(4,1)S(1)}, pred[16]{0:T(512)(128)(4,1)}, u32[]{:S(2)}) copy-start(pred[16]{0:T(512)(128)(4,1)} %copy-done.16) | copy-start | bytes 52
  122.5 26.7 %all-to-all-start.2 = ((bf16[16,2,5376]{2,1,0:T(2,128)(2,1)}), bf16[16,2,5376]{2,1,0:T(2,128)(2,1)}, u32[]{:S(2)}, u32[]{:S(2)}) async-start(bf16[16,2,5376]{2,1,0:T(2,128)(2,1)} %reshape.230), calls=%async_computation.2 | async-start | bytes 688128 | tf_op jit(solution)/shard_map/all_to_all | solution.py:61
  168.3 15.1 %copy-start.15 = (pred[16]{0:T(512)(128)(4,1)S(1)}, pred[16]{0:T(512)(128)(4,1)}, u32[]{:S(2)}) copy-start(pred[16]{0:T(512)(128)(4,1)} %copy-done.14) | copy-start | bytes 52
  176.9 10.3 %copy-start.13 = (pred[16]{0:T(512)(128)(4,1)S(1)}, pred[16]{0:T(512)(128)(4,1)}, u32[]{:S(2)}) copy-start(pred[16]{0:T(512)(128)(4,1)} %copy-done.12) | copy-start | bytes 52
  179.2 17.2 %all-to-all-start.3 = ((bf16[4,336,128]{2,0,1:T(4,128)(2,1)}), bf16[4,336,128]{2,0,1:T(4,128)(2,1)}, u32[]{:S(2)}, u32[]{:S(2)}) async-start(bf16[4,336,128]{2,0,1:T(4,128)(2,1)} %copy.104), calls=%async_computation.3 | async-start | bytes 688128 | tf_op jit(solution)/shard_map/all_to_all | solution.py:62
  185.9 4.9 %copy-start.25 = (pred[128]{0:T(512)(128)(4,1)S(1)}, pred[128]{0:T(512)(128)(4,1)}, u32[]{:S(2)}) copy-start(pred[128]{0:T(512)(128)(4,1)} %get-tuple-element.15) | copy-start | bytes 388
  189.0 8.6 %copy-start.2 = (f32[4,21,2048]{2,1,0:T(8,128)S(1)}, f32[4,21,2048]{2,1,0:T(8,128)}, u32[]{:S(2)}) copy-start(f32[4,21,2048]{2,1,0:T(8,128)} %copy-done.1) | copy-start | bytes 2064388
  (2 other events, 1.6 us)
Sparse Core Ops, SparseCore 0:
  10.4 77.3 all-gather.1
  115.2 64.2 reduce-scatter.1
where the time goes:
time: 207 us; the launch traced here: 206 us
  local copies, waits for them, and re-layouts  75.1 us (36%)
  waiting for transfers between devices  48 us (23%)
  starting transfers between devices  33.7 us (16%)
  matrix products  25 us (12%)
  between operations  15.4 us (7%)
  other arithmetic  8.7 us (4%)
    unnamed x62, local copies, waits for them, and re-layouts  25.2 us
    all_to_all x2, starting transfers between devices, per_device(): lax.all_to_all(scaled, 'tm', split_axis=2, concat_axis=1, tiled=True)  23.1 us
    all_to_all x2, waiting for transfers between devices, per_device(): lax.all_to_all(scaled, 'tm', split_axis=2, concat_axis=1, tiled=True)  21.6 us
    dot_general x12, matrix products, network_term(): lax.dot_general(picked, link_blocks[link], (((2,), (1,)), ((0,), (0,))),...  18.5 us
    gather x12, local copies, waits for them, and re-layouts, network_term(): picked = jnp.take(zone_major, zone_links[:, link], axis=0)  15.8 us
    all_gather x1, waiting for transfers between devices, per_device(): all_blocks = lax.all_gather(blocks, 'tm', axis=0, tiled=True)  13.9 us
    all_to_all x2, waiting for transfers between devices, per_device(): lax.all_to_all(temporal_term(moved, masked_turned), 'tm', split_axis=1, c...  11.7 us
    all_to_all x2, starting transfers between devices, per_device(): lax.all_to_all(temporal_term(moved, masked_turned), 'tm', split_axis=1, c...  10.4 us
  transfers between devices with their start and end apart: 6, of which 5 were waited for; matrix products, arithmetic and copies ran while one was open for 38% of the time, Pallas kernels for 0%

commit v1 on v0

--- a/solution.py
+++ b/solution.py
@@ -41,7 +41,9 @@
 
 
 def per_device(cotangent, blocks, zone_links, step_size, coupling, ramp_band, candidates):
-    all_blocks = lax.all_gather(blocks, "tm", axis=0, tiled=True)
+    all_blocks = jnp.concatenate(
+        lax.all_to_all(jnp.stack([blocks] * lax.axis_size("tm")), "tm", 0, 0), axis=0
+    )
     link_blocks = jnp.transpose(all_blocks, (1, 0, 2, 3))
     hour_count = coupling.shape[1]
     hour_ids = jnp.arange(hour_count, dtype=jnp.int32)

time: 207 us -> 258 us (1.25)
  the two profiles are of different devices: /device:TPU:24 before, /device:TPU:48 now
where the time goes in v1:
time: 258 us; the launch traced here: 257 us
  waiting for transfers between devices  89.2 us (35%)
  local copies, waits for them, and re-layouts  79.2 us (31%)
  starting transfers between devices  24.8 us (10%)
  matrix products  21.6 us (8%)
  blocking collectives  17.6 us (7%)
  between operations  15.4 us (6%)
  other arithmetic  8.74 us (3%)
    all_to_all x1, waiting for transfers between devices, per_device(): lax.all_to_all(jnp.stack([blocks] * lax.axis_size('tm')), 'tm', 0, 0)  67 us
    unnamed x66, local copies, waits for them, and re-layouts  25.3 us
    all_to_all x2, waiting for transfers between devices, per_device(): lax.all_to_all(scaled, 'tm', split_axis=2, concat_axis=1, tiled=True)  18.4 us
    all_to_all x1, blocking collectives, per_device(): lax.all_to_all(temporal_term(moved, masked_turned), 'tm', split_axis=1, c...  17.6 us
    gather x12, local copies, waits for them, and re-layouts, network_term(): picked = jnp.take(zone_major, zone_links[:, link], axis=0)  15.9 us
    all_to_all x2, starting transfers between devices, per_device(): lax.all_to_all(scaled, 'tm', split_axis=2, concat_axis=1, tiled=True)  15.4 us
    dot_general x12, matrix products, network_term(): lax.dot_general(picked, link_blocks[link], (((2,), (1,)), ((0,), (0,))),...  15.1 us
    slice x10, local copies, waits for them, and re-layouts, temporal_term(): column = moved[scen, :, 0:bus_width]  7.2 us
  transfers between devices with their start and end apart: 5, of which 4 were waited for; matrix products, arithmetic and copies ran while one was open for 25% of the time, Pallas kernels for 0%

profile of v1, /device:TPU:48, one launch (start us, length us, event | category | flops | bytes accessed | tf_op | source)
XLA Modules:
  0.0 256.6 jit_solution(9436417648071570737)
XLA Ops:
  10.1 4.2 %reshape.235 = bf16[16,2,5376]{2,1,0:T(2,128)(2,1)} reshape(bf16[2048,4,21]{2,1,0:T(4,128)(2,1)S(1)} %bitcast.152) | data formatting | bytes 688128
  14.3 10.1 %all-to-all-start.1 = ((bf16[16,2,5376]{2,1,0:T(2,128)(2,1)}), bf16[16,2,5376]{2,1,0:T(2,128)(2,1)S(1)}, u32[]{:S(2)}, u32[]{:S(2)}) async-start(bf16[16,2,5376]{2,1,0:T(2,128)(2,1)} %reshape.235), calls=%async_computation.1 | async-start | bytes 688128 | tf_op jit(solution)/shard_map/all_to_all | solution.py:63
  25.1 13.4 %all-to-all-done.1 = bf16[16,2,5376]{2,1,0:T(2,128)(2,1)S(1)} async-done(((bf16[16,2,5376]{2,1,0:T(2,128)(2,1)}), bf16[16,2,5376]{2,1,0:T(2,128)(2,1)S(1)}, u32[]{:S(2)}, u32[]{:S(2)}) %all-to-all-start.1) | async-done | bytes 344096 | tf_op jit(solution)/shard_map/all_to_all | solution.py:63
  38.5 5.1 %reshape.236 = bf16[2048,4,21]{2,1,0:T(4,128)(2,1)S(1)} reshape(bf16[16,2,5376]{2,1,0:T(2,128)(2,1)S(1)} %all-to-all-done.1) | data formatting | bytes 688128
  46.8 17.6 %all_to_all.53 = bf16[4,336,128]{2,0,1:T(4,128)(2,1)S(1)} all-to-all(bf16[4,336,128]{2,0,1:T(4,128)(2,1)S(1)} %copy.90), channel_id=1, replica_groups=mesh['scen'=16,'tm'=16] {'tm'}, dimensions={1} | all-to-all | bytes 688128 | tf_op jit(solution)/shard_map/all_to_all | solution.py:64
  64.4 2.5 stack.59
  66.9 4.6 %all-to-all-start = ((bf16[16,1,6,128,128]{4,3,2,1,0:T(8,128)(2,1)}), bf16[16,1,6,128,128]{4,3,2,1,0:T(8,128)(2,1)}, u32[]{:S(2)}, u32[]{:S(2)}) async-start(bf16[16,1,6,128,128]{4,3,2,1,0:T(8,128)(2,1)} %stack.59), calls=%async_computation | async-start | bytes 6291456 | tf_op jit(solution)/shard_map/all_to_all | solution.py:45
  81.9 67.0 %all-to-all-done = bf16[16,1,6,128,128]{4,3,2,1,0:T(8,128)(2,1)} async-done(((bf16[16,1,6,128,128]{4,3,2,1,0:T(8,128)(2,1)}), bf16[16,1,6,128,128]{4,3,2,1,0:T(8,128)(2,1)}, u32[]{:S(2)}, u32[]{:S(2)}) %all-to-all-start) | async-done | bytes 3145760 | tf_op jit(solution)/shard_map/all_to_all | solution.py:45
  148.9 2.2 copy.125
  154.7 2.1 reshape.85
  156.8 2.9 %multiply_reduce_fusion = (f32[21,2048]{1,0:T(8,128)}, f32[21,2048]{1,0:T(8,128)}, f32[4,21,2048]{2,1,0:T(8,128)S(1)}) fusion(f32[2048]{0:T(1024)S(1)} %copy-done.9, f32[4,21,2048]{2,0,1:T(4,128)} %param.9, f32[4,21,2048]{2,1,0:T(8,128)} %reshape.233, f32[4,21,2048]{2,1,0:T(8,128)} %reshape.85), kind=kLoop, calls=%fused_computation.48 | loop fusion | flops 946176 | bytes 3104768 | tf_op jit(solution)/shard_map/reduce_sum | solution.py:60
  169.3 4.0 %copy.95 = bf16[4,21,2048]{1,0,2:T(4,128)(2,1)} copy(bf16[4,21,2048]{2,1,0:T(8,128)(2,1)} %copy-done.2) | data formatting | bytes 688128 | tf_op jit(solution)/shard_map/convert_element_type | solution.py:62
  173.3 1.7 add_multiply_fusion
  175.1 2.2 fusion.14
  177.3 5.1 %reshape.237 = bf16[16,2,5376]{2,1,0:T(2,128)(2,1)} reshape(bf16[2048,4,21]{2,1,0:T(4,128)(2,1)} %bitcast.149) | data formatting | bytes 688128
  182.4 5.2 %all-to-all-start.3 = ((bf16[16,2,5376]{2,1,0:T(2,128)(2,1)}), bf16[16,2,5376]{2,1,0:T(2,128)(2,1)}, u32[]{:S(2)}, u32[]{:S(2)}) async-start(bf16[16,2,5376]{2,1,0:T(2,128)(2,1)} %reshape.237), calls=%async_computation.3 | async-start | bytes 688128 | tf_op jit(solution)/shard_map/all_to_all | solution.py:63
  187.7 2.5 convolution_add_fusion.4
  191.5 1.6 convolution_add_fusion.3
  193.2 2.3 convolution_add_fusion.2
  195.4 5.0 %all-to-all-done.3 = bf16[16,2,5376]{2,1,0:T(2,128)(2,1)} async-done(((bf16[16,2,5376]{2,1,0:T(2,128)(2,1)}), bf16[16,2,5376]{2,1,0:T(2,128)(2,1)}, u32[]{:S(2)}, u32[]{:S(2)}) %all-to-all-start.3) | async-done | bytes 344096 | tf_op jit(solution)/shard_map/all_to_all | solution.py:63
  200.4 7.1 %reshape.238 = bf16[2048,4,21]{2,1,0:T(4,128)(2,1)} reshape(bf16[16,2,5376]{2,1,0:T(2,128)(2,1)} %all-to-all-done.3) | data formatting | bytes 688128
  207.5 3.4 %copy.109 = bf16[4,21,16,128]{3,2,0,1:T(8,128)(2,1)} copy(bf16[4,21,16,128]{1,0,3,2:T(4,128)(2,1)} %bitcast.151) | data formatting | bytes 688128 | tf_op jit(solution)/shard_map/all_to_all | solution.py:63
  210.9 1.7 fusion.74
  213.3 1.6 squeeze.99
  214.9 1.6 copy.98
  216.4 1.6 squeeze.100
  219.6 1.6 squeeze.101
  222.7 1.6 squeeze.102
  230.5 4.6 %all-to-all-start.4 = ((bf16[4,336,128]{2,0,1:T(4,128)(2,1)}), bf16[4,336,128]{2,0,1:T(4,128)(2,1)}, u32[]{:S(2)}, u32[]{:S(2)}) async-start(bf16[4,336,128]{2,0,1:T(4,128)(2,1)} %copy.101), calls=%async_computation.4 | async-start | bytes 688128 | tf_op jit(solution)/shard_map/all_to_all | solution.py:64
  235.1 2.5 convolution_add_fusion.1
  238.9 1.6 fusion
  243.3 3.8 %all-to-all-done.4 = bf16[4,336,128]{2,0,1:T(4,128)(2,1)} async-done(((bf16[4,336,128]{2,0,1:T(4,128)(2,1)}), bf16[4,336,128]{2,0,1:T(4,128)(2,1)}, u32[]{:S(2)}, u32[]{:S(2)}) %all-to-all-start.4) | async-done | bytes 344096 | tf_op jit(solution)/shard_map/all_to_all | solution.py:64
  (134 shorter events, 47.3 us)
Async XLA Ops:
  14.3 24.2 %all-to-all-start.1 = ((bf16[16,2,5376]{2,1,0:T(2,128)(2,1)}), bf16[16,2,5376]{2,1,0:T(2,128)(2,1)S(1)}, u32[]{:S(2)}, u32[]{:S(2)}) async-start(bf16[16,2,5376]{2,1,0:T(2,128)(2,1)} %reshape.235), calls=%async_computation.1 | async-start | bytes 688128 | tf_op jit(solution)/shard_map/all_to_all | solution.py:63
  25.1 20.3 %copy-start.29 = (bf16[1,336,336]{2,1,0:T(8,128)(2,1)S(1)}, bf16[1,336,336]{2,1,0:T(8,128)(2,1)}, u32[]{:S(2)}) copy-start(bf16[1,336,336]{2,1,0:T(8,128)(2,1)} %param.13) | copy-start | bytes 677380
  45.3 19.1 %copy-start.8 = (bf16[1,6,128,128]{3,2,1,0:T(8,128)(2,1)S(1)}, bf16[1,6,128,128]{3,2,1,0:T(8,128)(2,1)}, u32[]{:S(2)}) copy-start(bf16[1,6,128,128]{3,2,1,0:T(8,128)(2,1)} %param.10) | copy-start | bytes 589828
  66.9 5.2 %copy-start.26 = (s32[16,6]{0,1:T(8,128)S(1)}, s32[16,6]{0,1:T(8,128)}, u32[]{:S(2)}) copy-start(s32[16,6]{0,1:T(8,128)} %param.11) | copy-start | bytes 1156
  66.9 82.0 %all-to-all-start = ((bf16[16,1,6,128,128]{4,3,2,1,0:T(8,128)(2,1)}), bf16[16,1,6,128,128]{4,3,2,1,0:T(8,128)(2,1)}, u32[]{:S(2)}, u32[]{:S(2)}) async-start(bf16[16,1,6,128,128]{4,3,2,1,0:T(8,128)(2,1)} %stack.59), calls=%async_computation | async-start | bytes 6291456 | tf_op jit(solution)/shard_map/all_to_all | solution.py:45
  71.5 8.2 %copy-start.28 = (s32[128]{0:T(128)S(1)}, s32[128]{0:T(128)}, u32[]{:S(2)}) copy-start(s32[128]{0:T(128)} %param.15) | copy-start | bytes 1540
  71.5 169.3 %reduce-scatter.2.cloned.1.call-start = ((), (), s32[]{:S(2)}) async-start(), calls=%async_computation.6 | async-start | bytes 208896 | tf_op jit(solution)/shard_map/reduce_scatter | solution.py:69
  72.1 79.0 %copy-start.24 = (pred[16]{0:T(512)(128)(4,1)}, pred[16]{0:T(512)(128)(4,1)S(1)}, u32[]{:S(2)}) copy-start(pred[16]{0:T(512)(128)(4,1)S(1)} %get-tuple-element.44) | copy-start | bytes 52
  72.1 79.4 %copy-start.22 = (pred[16]{0:T(512)(128)(4,1)}, pred[16]{0:T(512)(128)(4,1)S(1)}, u32[]{:S(2)}) copy-start(pred[16]{0:T(512)(128)(4,1)S(1)} %get-tuple-element.42) | copy-start | bytes 52
  72.1 79.8 %copy-start.20 = (pred[16]{0:T(512)(128)(4,1)}, pred[16]{0:T(512)(128)(4,1)S(1)}, u32[]{:S(2)}) copy-start(pred[16]{0:T(512)(128)(4,1)S(1)} %get-tuple-element.40) | copy-start | bytes 52
  72.1 80.3 %copy-start.18 = (pred[16]{0:T(512)(128)(4,1)}, pred[16]{0:T(512)(128)(4,1)S(1)}, u32[]{:S(2)}) copy-start(pred[16]{0:T(512)(128)(4,1)S(1)} %get-tuple-element.38) | copy-start | bytes 52
  72.1 80.7 %copy-start.16 = (pred[16]{0:T(512)(128)(4,1)}, pred[16]{0:T(512)(128)(4,1)S(1)}, u32[]{:S(2)}) copy-start(pred[16]{0:T(512)(128)(4,1)S(1)} %get-tuple-element.46) | copy-start | bytes 52
  72.1 81.2 %copy-start.14 = (pred[16]{0:T(512)(128)(4,1)}, pred[16]{0:T(512)(128)(4,1)S(1)}, u32[]{:S(2)}) copy-start(pred[16]{0:T(512)(128)(4,1)S(1)} %get-tuple-element.18) | copy-start | bytes 52
  72.2 8.7 %copy-start.10 = (s32[1024]{0:T(1024)}, s32[1024]{0:T(1024)S(1)}, u32[]{:S(2)}) copy-start(s32[1024]{0:T(1024)S(1)} %get-tuple-element.52) | copy-start | bytes 12292
  72.2 8.6 %copy-start.11 = (s32[1024]{0:T(1024)}, s32[1024]{0:T(1024)S(1)}, u32[]{:S(2)}) copy-start(s32[1024]{0:T(1024)S(1)} %get-tuple-element.53) | copy-start | bytes 12292
  74.2 6.7 %copy-start.12 = (s32[1024]{0:T(1024)}, s32[1024]{0:T(1024)S(1)}, u32[]{:S(2)}) copy-start(s32[1024]{0:T(1024)S(1)} %get-tuple-element.50) | copy-start | bytes 12292
  76.9 3.9 %copy-start.13 = (s32[1024]{0:T(1024)}, s32[1024]{0:T(1024)S(1)}, u32[]{:S(2)}) copy-start(s32[1024]{0:T(1024)S(1)} %get-tuple-element.49) | copy-start | bytes 12292
  148.9 2.2 copy-start.7
  151.1 1.4 copy-start.3
  151.5 1.4 copy-start.6
  152.0 1.3 copy-start.5
  153.3 3.5 %copy-start.9 = (f32[2048]{0:T(1024)S(1)}, f32[2048]{0:T(1024)}, u32[]{:S(2)}) copy-start(f32[2048]{0:T(1024)} %param.12) | copy-start | bytes 24580
  163.4 11.6 %copy-start.25 = (pred[16]{0:T(512)(128)(4,1)S(1)}, pred[16]{0:T(512)(128)(4,1)}, u32[]{:S(2)}) copy-start(pred[16]{0:T(512)(128)(4,1)} %copy-done.24) | copy-start | bytes 52
  173.3 14.4 %copy-start.23 = (pred[16]{0:T(512)(128)(4,1)S(1)}, pred[16]{0:T(512)(128)(4,1)}, u32[]{:S(2)}) copy-start(pred[16]{0:T(512)(128)(4,1)} %copy-done.22) | copy-start | bytes 52
  177.3 14.2 %copy-start.21 = (pred[16]{0:T(512)(128)(4,1)S(1)}, pred[16]{0:T(512)(128)(4,1)}, u32[]{:S(2)}) copy-start(pred[16]{0:T(512)(128)(4,1)} %copy-done.20) | copy-start | bytes 52
  182.4 10.7 %copy-start.19 = (pred[16]{0:T(512)(128)(4,1)S(1)}, pred[16]{0:T(512)(128)(4,1)}, u32[]{:S(2)}) copy-start(pred[16]{0:T(512)(128)(4,1)} %copy-done.18) | copy-start | bytes 52
  182.4 18.0 %all-to-all-start.3 = ((bf16[16,2,5376]{2,1,0:T(2,128)(2,1)}), bf16[16,2,5376]{2,1,0:T(2,128)(2,1)}, u32[]{:S(2)}, u32[]{:S(2)}) async-start(bf16[16,2,5376]{2,1,0:T(2,128)(2,1)} %reshape.237), calls=%async_computation.3 | async-start | bytes 688128 | tf_op jit(solution)/shard_map/all_to_all | solution.py:63
  219.6 15.5 %copy-start.17 = (pred[16]{0:T(512)(128)(4,1)S(1)}, pred[16]{0:T(512)(128)(4,1)}, u32[]{:S(2)}) copy-start(pred[16]{0:T(512)(128)(4,1)} %copy-done.16) | copy-start | bytes 52
  228.2 10.7 %copy-start.15 = (pred[16]{0:T(512)(128)(4,1)S(1)}, pred[16]{0:T(512)(128)(4,1)}, u32[]{:S(2)}) copy-start(pred[16]{0:T(512)(128)(4,1)} %copy-done.14) | copy-start | bytes 52
  230.5 16.6 %all-to-all-start.4 = ((bf16[4,336,128]{2,0,1:T(4,128)(2,1)}), bf16[4,336,128]{2,0,1:T(4,128)(2,1)}, u32[]{:S(2)}, u32[]{:S(2)}) async-start(bf16[4,336,128]{2,0,1:T(4,128)(2,1)} %copy.101), calls=%async_computation.4 | async-start | bytes 688128 | tf_op jit(solution)/shard_map/all_to_all | solution.py:64
  237.6 4.9 %copy-start.27 = (pred[128]{0:T(512)(128)(4,1)S(1)}, pred[128]{0:T(512)(128)(4,1)}, u32[]{:S(2)}) copy-start(pred[128]{0:T(512)(128)(4,1)} %get-tuple-element.15) | copy-start | bytes 388
  240.7 7.6 %copy-start.1 = (f32[4,21,2048]{2,1,0:T(8,128)S(1)}, f32[4,21,2048]{2,1,0:T(8,128)}, u32[]{:S(2)}) copy-start(f32[4,21,2048]{2,1,0:T(8,128)} %copy-done) | copy-start | bytes 2064388
  (3 other events, 2.6 us)
Sparse Core Ops, SparseCore 0:
  175.2 54.4 reduce-scatter.1
